TPU v7x, 32 devices: a whole 2x2x4 slice. The times are simulated.
32 devices in a mesh: fsdp: 2 (over core), context: 4 (over y, x), tensor: 4 (over z).
Axes of the slice: x: 2, y: 2, z: 4, core: 2. Of those that a mesh axis runs over, the one named last changes fastest.
Arguments:
- inputs: bfloat16 [2, 2, 1280, 2048], P(None, 'fsdp', ('context', 'tensor')), may hold values from -6 to 6
- segments: int32 [2, 2, 1280], P(None, 'fsdp'), may hold values from 0 to 7, never falling along the last dimension, each value on 1 to 640 neighbouring positions
- norm_gain: float32 [2048], replicated, may hold values from 0.5 to 1.5
- branch_weight: bfloat16 [2048, 2560], P(('fsdp', 'context'), 'tensor'), may hold values from -0.125 to 0.125
- inner_weight: bfloat16 [2048, 2560], P(('fsdp', 'context'), 'tensor'), may hold values from -0.125 to 0.125
- conv_weight: float32 [4, 2560], P(None, 'tensor'), may hold values from -3 to 3
- conv_bias: float32 [2560], P('tensor'), may hold values from -3 to 3
- rate_weight: bfloat16 [16, 160, 160], P('tensor'), may hold values from -0.5 to 0.5
- rate_bias: float32 [2560], P('tensor'), may hold values from -4 to 4
- input_weight: bfloat16 [16, 160, 160], P('tensor'), may hold values from -0.5 to 0.5
- input_bias: float32 [2560], P('tensor'), may hold values from -4 to 4
- decay_param: float32 [2560], P('tensor'), may hold values from 4 to 11
- out_weight: bfloat16 [2560, 2048], P('tensor', ('fsdp', 'context')), may hold values from -0.5 to 0.5
- mlp_gain: float32 [2048], replicated, may hold values from 0.5 to 1.5
- gate_weight: bfloat16 [2048, 6144], P(('fsdp', 'context'), 'tensor'), may hold values from -0.125 to 0.125
- up_weight: bfloat16 [2048, 6144], P(('fsdp', 'context'), 'tensor'), may hold values from -0.125 to 0.125
- down_weight: bfloat16 [6144, 2048], P('tensor', ('fsdp', 'context')), may hold values from -0.15625 to 0.15625
- cotangent: bfloat16 [2, 2, 1280, 2048], P(None, 'fsdp', ('context', 'tensor')), may hold values from -6 to 6
Outputs:
- block_out: bfloat16 [2, 2, 1280, 2048], P(None, 'fsdp', ('context', 'tensor'))
- input_grad: float32 [2, 2, 1280, 2048], P(None, 'fsdp', ('context', 'tensor'))
- norm_gain_grad: float32 [2048], replicated
- branch_weight_grad: float32 [2048, 2560], P(('fsdp', 'context'), 'tensor')
- inner_weight_grad: float32 [2048, 2560], P(('fsdp', 'context'), 'tensor')
- conv_weight_grad: float32 [4, 2560], P(None, 'tensor')
- conv_bias_grad: float32 [2560], P('tensor')
- rate_weight_grad: float32 [16, 160, 160], P('tensor')
- rate_bias_grad: float32 [2560], P('tensor')
- input_weight_grad: float32 [16, 160, 160], P('tensor')
- input_bias_grad: float32 [2560], P('tensor')
- decay_param_grad: float32 [2560], P('tensor')
- out_weight_grad: float32 [2560, 2048], P('tensor', ('fsdp', 'context'))
- mlp_gain_grad: float32 [2048], replicated
- gate_weight_grad: float32 [2048, 6144], P(('fsdp', 'context'), 'tensor')
- up_weight_grad: float32 [2048, 6144], P(('fsdp', 'context'), 'tensor')
- down_weight_grad: float32 [6144, 2048], P('tensor', ('fsdp', 'context'))
Inputs may be any that keep to these rules, and one draw needn't show every extreme that they name: `segments`: along each sequence the numbers never fall; each document is one run of 1 to 640 positions, every number of 0 to 7 is used in each sequence, and one document of each sequence has exactly 640 positions.
All inputs are finite; a program needn't handle non-finite values.
Results may differ from a plain program's by a relative error of at most 0.014.
Values may be sent and summed in bfloat16 or wider, within the bound.
No kernel may reach another device: no remote copies, remote signals or barrier semaphores. Data moves between devices by JAX's collectives and lax.ppermute only.
A program may use at most 256 MiB of HBM per device.

v0:
```python
from functools import partial
import jax
import jax.numpy as jnp
from jax import lax
from jax.sharding import PartitionSpec as P

CONV = 4
CPOW = 8
EPS = 1e-06


def from_behind(value, axis, by):
    length = lax.axis_size(axis)
    pairs = [(i, i + by) for i in range(length) if 0 <= i + by < length]
    return lax.ppermute(value, axis, pairs)


def rms_norm(values, gain_vec):
    return values * lax.rsqrt(jnp.mean(values * values, axis=-1, keepdims=True) + EPS) * gain_vec


def round_low(values):
    return lax.optimization_barrier(values.astype(jnp.bfloat16)).astype(jnp.float32)


def combine(earlier, following):
    return (earlier[0] * following[0], following[0] * earlier[1] + following[1])


def local_scan(coeffs, offsets):
    return lax.associative_scan(combine, (coeffs, offsets), axis=1)


def gate_terms(rate_pre, input_pre, conv_vals, decay_param, starts):
    log_rate = -CPOW * jax.nn.softplus(-decay_param) * jax.nn.sigmoid(rate_pre)
    decays = jnp.where(starts, 0.0, jnp.exp(log_rate))
    input_scale = jnp.where(starts, 1.0, jnp.sqrt(-jnp.expm1(2.0 * log_rate)))
    return (decays, input_scale * jax.nn.sigmoid(input_pre) * conv_vals)


def gated_unit(gate_pre, up_pre):
    return jax.nn.gelu(gate_pre) * up_pre


def conv_mix(extended, conv_w, conv_b, same_masks):
    length_rows = extended.shape[1] - (CONV - 1)
    total = conv_b + conv_w[0] * extended[:, CONV - 1 :]
    for offset in range(1, CONV):
        total = (
            total
            + conv_w[offset]
            * extended[:, CONV - 1 - offset : CONV - 1 - offset + length_rows]
            * same_masks[offset - 1]
        )
    return total


def project(rows_in, weight):
    return jnp.einsum("sla,ab->slb", rows_in, weight, preferred_element_type=jnp.float32)


def project_back(grad_vals, weight):
    return jnp.einsum("slb,ab->sla", grad_vals, weight, preferred_element_type=jnp.float32)


def outer_sum(rows_in, grad_vals):
    return jnp.einsum("sla,slb->ab", rows_in, grad_vals, preferred_element_type=jnp.float32)


def split_blocks(values, weight):
    return values.reshape(values.shape[0], values.shape[1], weight.shape[0], weight.shape[1])


def block_mix(values, weight):
    return jnp.einsum(
        "slnb,nbc->slnc", split_blocks(values, weight), weight, preferred_element_type=jnp.float32
    ).reshape(values.shape)


def block_back(grad_vals, weight):
    return jnp.einsum(
        "slnc,nbc->slnb",
        split_blocks(grad_vals, weight),
        weight,
        preferred_element_type=jnp.float32,
    ).reshape(grad_vals.shape)


def block_outer(values, grad_vals, weight):
    return jnp.einsum(
        "slnb,slnc->nbc",
        split_blocks(values, weight),
        split_blocks(grad_vals, weight),
        preferred_element_type=jnp.float32,
    )


def fetch_weights(branch_w, inner_w, gate_w, up_w, out_w, down_w):
    return (
        lax.all_gather(branch_w, ("fsdp", "context"), axis=0, tiled=True),
        lax.all_gather(inner_w, ("fsdp", "context"), axis=0, tiled=True),
        lax.all_gather(gate_w, ("fsdp", "context"), axis=0, tiled=True),
        lax.all_gather(up_w, ("fsdp", "context"), axis=0, tiled=True),
        lax.all_gather(out_w, ("fsdp", "context"), axis=1, tiled=True),
        lax.all_gather(down_w, ("fsdp", "context"), axis=1, tiled=True),
    )


def widen_rows(values):
    return lax.all_gather(values, "tensor", axis=1, tiled=True)


def narrow_rows(partial_vals):
    return lax.psum_scatter(partial_vals, "tensor", scatter_dimension=1, tiled=True)


def widen_grads(values):
    return lax.all_gather(values, "tensor", axis=1, tiled=True)


def narrow_grads(partial_vals):
    return lax.psum_scatter(partial_vals, "tensor", scatter_dimension=1, tiled=True)


def carry_state(coeffs, offsets, reverse):
    incoming = jnp.zeros_like(offsets)
    direction = -1 if reverse else 1
    for relay_turn in range(lax.axis_size("context") - 1):
        incoming = from_behind(coeffs * incoming + offsets, "context", direction)
    return incoming


def per_device(
    inputs,
    segments,
    norm_gain,
    branch_weight,
    inner_weight,
    conv_weight,
    conv_bias,
    rate_weight,
    rate_bias,
    input_weight,
    input_bias,
    decay_param,
    out_weight,
    mlp_gain,
    gate_weight,
    up_weight,
    down_weight,
    cotangent,
):
    seq_count = inputs.shape[1]
    span_rows = inputs.shape[2] * lax.axis_size("tensor")
    context_pos = lax.axis_index("context")
    halo_rows = CONV - 1
    lead_pad = jnp.full((seq_count, halo_rows), -1, jnp.int32)
    totals = None
    block_outs = []
    input_grads = []
    for micro_idx in range(inputs.shape[0]):
        gathered = fetch_weights(
            branch_weight, inner_weight, gate_weight, up_weight, out_weight, down_weight
        )
        full_branch, full_inner, full_gate, full_up, full_out, full_down = gathered
        seg_ext = lax.dynamic_slice_in_dim(
            jnp.concatenate([lead_pad, segments[micro_idx]], axis=1),
            context_pos * span_rows,
            span_rows + halo_rows,
            axis=1,
        )
        current = seg_ext[:, halo_rows:]
        same_masks = [
            (seg_ext[:, halo_rows - offset : halo_rows - offset + span_rows] == current).astype(
                jnp.float32
            )[:, :, None]
            for offset in range(1, CONV)
        ]
        starts = (seg_ext[:, halo_rows - 1 : halo_rows - 1 + span_rows] != current)[:, :, None]
        x_rows = inputs[micro_idx].astype(jnp.float32)
        normed_one, norm_one_back = jax.vjp(rms_norm, x_rows, norm_gain)
        wide_one = widen_rows(normed_one.astype(jnp.bfloat16))
        branch_pre = project(wide_one, full_branch)
        inner_low = project(wide_one, full_inner).astype(jnp.bfloat16)
        edge_rows = from_behind(inner_low[:, span_rows - halo_rows :], "context", 1)
        extended = jnp.concatenate([edge_rows, inner_low], axis=1).astype(jnp.float32)
        conv_out, conv_back = jax.vjp(
            partial(conv_mix, same_masks=same_masks), extended, conv_weight, conv_bias
        )
        conv_low = conv_out.astype(jnp.bfloat16)
        rate_pre = block_mix(conv_low, rate_weight) + rate_bias
        input_pre = block_mix(conv_low, input_weight) + input_bias
        (decays, drives), gate_back = jax.vjp(
            partial(gate_terms, starts=starts),
            rate_pre,
            input_pre,
            conv_low.astype(jnp.float32),
            decay_param,
        )
        prod_loc, state_loc = local_scan(decays, drives)
        state_in = carry_state(prod_loc[:, -1], state_loc[:, -1], False)
        states = state_loc + prod_loc * state_in[:, None]
        gelu_branch, gelu_back = jax.vjp(jax.nn.gelu, branch_pre)
        mixed_low = (states * gelu_branch).astype(jnp.bfloat16)
        residual = x_rows + narrow_rows(project(mixed_low, full_out))
        normed_two, norm_two_back = jax.vjp(rms_norm, residual, mlp_gain)
        wide_two = widen_rows(normed_two.astype(jnp.bfloat16))
        gate_pre = project(wide_two, full_gate)
        up_pre = project(wide_two, full_up)
        hidden_val, hidden_back = jax.vjp(gated_unit, gate_pre, up_pre)
        hidden_low = hidden_val.astype(jnp.bfloat16)
        block_outs.append(
            (residual + narrow_rows(project(hidden_low, full_down))).astype(jnp.bfloat16)
        )
        out_grad = cotangent[micro_idx].astype(jnp.float32)
        wide_grad = widen_grads(cotangent[micro_idx])
        down_term = outer_sum(hidden_low, wide_grad)
        gate_grad, up_grad = hidden_back(project_back(wide_grad, full_down))
        gate_low = gate_grad.astype(jnp.bfloat16)
        up_low = up_grad.astype(jnp.bfloat16)
        gate_term = outer_sum(wide_two, gate_low)
        up_term = outer_sum(wide_two, up_low)
        normed_two_grad = round_low(
            narrow_grads(project_back(gate_low, full_gate) + project_back(up_low, full_up))
        )
        resid_norm_grad, gain_two_term = norm_two_back(normed_two_grad)
        resid_grad = out_grad + resid_norm_grad
        wide_resid = widen_grads(resid_grad.astype(jnp.bfloat16))
        out_term = outer_sum(mixed_low, wide_resid)
        mixed_grad = project_back(wide_resid, full_out)
        (branch_grad,) = gelu_back(mixed_grad * states)
        branch_low = branch_grad.astype(jnp.bfloat16)
        state_grad = mixed_grad * gelu_branch
        next_decays = jnp.concatenate([decays[:, 1:], jnp.ones_like(decays[:, :1])], axis=1)
        rev_prod, rev_grad = local_scan(jnp.flip(next_decays, 1), jnp.flip(state_grad, 1))
        rev_prod = jnp.flip(rev_prod, 1)
        rev_grad = jnp.flip(rev_grad, 1)
        grad_in = carry_state(decays[:, 0] * rev_prod[:, 0], decays[:, 0] * rev_grad[:, 0], True)
        drive_grad = rev_grad + rev_prod * grad_in[:, None]
        prev_states = jnp.concatenate([state_in[:, None], states[:, :-1]], axis=1)
        rate_grad, input_pre_grad, conv_part, decay_term = gate_back(
            (drive_grad * prev_states, drive_grad)
        )
        rate_low = rate_grad.astype(jnp.bfloat16)
        input_low = input_pre_grad.astype(jnp.bfloat16)
        rate_w_term = block_outer(conv_low, rate_low, rate_weight)
        rate_b_term = jnp.sum(rate_low.astype(jnp.float32), axis=(0, 1))
        input_w_term = block_outer(conv_low, input_low, input_weight)
        input_b_term = jnp.sum(input_low.astype(jnp.float32), axis=(0, 1))
        conv_grad = (
            conv_part + block_back(rate_low, rate_weight) + block_back(input_low, input_weight)
        )
        ext_grad, conv_w_term, conv_b_term = conv_back(conv_grad)
        edge_grad = from_behind(ext_grad[:, :halo_rows], "context", -1)
        inner_grad = ext_grad[:, halo_rows:] + jnp.concatenate(
            [jnp.zeros_like(ext_grad[:, 2 * halo_rows :]), edge_grad], axis=1
        )
        inner_low_grad = inner_grad.astype(jnp.bfloat16)
        inner_term = outer_sum(wide_one, inner_low_grad)
        branch_term = outer_sum(wide_one, branch_low)
        normed_one_grad = round_low(
            narrow_grads(
                project_back(inner_low_grad, full_inner) + project_back(branch_low, full_branch)
            )
        )
        x_norm_grad, gain_one_term = norm_one_back(normed_one_grad)
        input_grads.append(resid_grad + x_norm_grad)
        terms = (
            gain_one_term,
            branch_term,
            inner_term,
            conv_w_term,
            conv_b_term,
            rate_w_term,
            rate_b_term,
            input_w_term,
            input_b_term,
            decay_term,
            out_term,
            gain_two_term,
            gate_term,
            up_term,
            down_term,
        )
        totals = terms if totals is None else jax.tree.map(jnp.add, totals, terms)
    big_grads = (
        lax.psum_scatter(
            totals[1].astype(jnp.bfloat16), ("fsdp", "context"), scatter_dimension=0, tiled=True
        ).astype(jnp.float32),
        lax.psum_scatter(
            totals[2].astype(jnp.bfloat16), ("fsdp", "context"), scatter_dimension=0, tiled=True
        ).astype(jnp.float32),
        lax.psum_scatter(
            totals[12].astype(jnp.bfloat16), ("fsdp", "context"), scatter_dimension=0, tiled=True
        ).astype(jnp.float32),
        lax.psum_scatter(
            totals[13].astype(jnp.bfloat16), ("fsdp", "context"), scatter_dimension=0, tiled=True
        ).astype(jnp.float32),
        lax.psum_scatter(
            totals[10].astype(jnp.bfloat16), ("fsdp", "context"), scatter_dimension=1, tiled=True
        ).astype(jnp.float32),
        lax.psum_scatter(
            totals[14].astype(jnp.bfloat16), ("fsdp", "context"), scatter_dimension=1, tiled=True
        ).astype(jnp.float32),
    )
    small_grads = (
        lax.psum(totals[3].astype(jnp.bfloat16), ("fsdp", "context")).astype(jnp.float32),
        lax.psum(totals[4].astype(jnp.bfloat16), ("fsdp", "context")).astype(jnp.float32),
        lax.psum(totals[5].astype(jnp.bfloat16), ("fsdp", "context")).astype(jnp.float32),
        lax.psum(totals[6].astype(jnp.bfloat16), ("fsdp", "context")).astype(jnp.float32),
        lax.psum(totals[7].astype(jnp.bfloat16), ("fsdp", "context")).astype(jnp.float32),
        lax.psum(totals[8].astype(jnp.bfloat16), ("fsdp", "context")).astype(jnp.float32),
        lax.psum(totals[9].astype(jnp.bfloat16), ("fsdp", "context")).astype(jnp.float32),
    )
    gain_grads = lax.psum((totals[0], totals[11]), ("fsdp", "context", "tensor"))
    return (
        jnp.stack(block_outs),
        jnp.stack(input_grads),
        gain_grads[0],
        big_grads[0],
        big_grads[1],
        small_grads[0],
        small_grads[1],
        small_grads[2],
        small_grads[3],
        small_grads[4],
        small_grads[5],
        small_grads[6],
        big_grads[4],
        gain_grads[1],
        big_grads[2],
        big_grads[3],
        big_grads[5],
    )


def solution(mesh):
    placed = (
        P(None, "fsdp", ("context", "tensor"), None),
        P(None, "fsdp", None),
        P(),
        P(("fsdp", "context"), "tensor"),
        P(("fsdp", "context"), "tensor"),
        P(None, "tensor"),
        P("tensor"),
        P("tensor", None, None),
        P("tensor"),
        P("tensor", None, None),
        P("tensor"),
        P("tensor"),
        P("tensor", ("fsdp", "context")),
        P(),
        P(("fsdp", "context"), "tensor"),
        P(("fsdp", "context"), "tensor"),
        P("tensor", ("fsdp", "context")),
        P(None, "fsdp", ("context", "tensor"), None),
    )
    return jax.shard_map(
        per_device,
        mesh=mesh,
        in_specs=placed,
        out_specs=(
            P(None, "fsdp", ("context", "tensor"), None),
            P(None, "fsdp", ("context", "tensor"), None),
            P(),
            P(("fsdp", "context"), "tensor"),
            P(("fsdp", "context"), "tensor"),
            P(None, "tensor"),
            P("tensor"),
            P("tensor", None, None),
            P("tensor"),
            P("tensor", None, None),
            P("tensor"),
            P("tensor"),
            P("tensor", ("fsdp", "context")),
            P(),
            P(("fsdp", "context"), "tensor"),
            P(("fsdp", "context"), "tensor"),
            P("tensor", ("fsdp", "context")),
        ),
        check_vma=False,
    )
```

profile of v0, /device:TPU:0, one launch (start us, length us, event | category | flops | bytes accessed | tf_op | source)
XLA Modules:
  0.0 2164.8 jit_solution(8397309703831230440)
XLA Ops:
  14.8 32.1 %all-gather.17.cloned.1.call-done = bf16[1,320,2048]{2,1,0:T(8,128)(2,1)} async-done(((bf16[1,80,2048]{2,1,0:T(8,128)(2,1)}), bf16[1,320,2048]{2,1,0:T(8,128)(2,1)}) %all-gather.17.cloned.1.call-update) | async-done | bytes 1310736 | tf_op jit(solution)/shard_map/all_gather | solution.py:110
  46.9 31.0 %all-gather.19.cloned.1.call-done = bf16[2048,640]{1,0:T(8,128)(2,1)} async-done(((bf16[256,640]{1,0:T(8,128)(2,1)}), bf16[2048,640]{1,0:T(8,128)(2,1)}) %all-gather.19.cloned.1.call-update) | async-done | bytes 2621456 | tf_op jit(solution)/shard_map/all_gather | solution.py:101
  84.8 28.0 %all-gather.33.cloned.1.call-done = bf16[1,320,2048]{2,1,0:T(8,128)(2,1)} async-done(((bf16[1,80,2048]{2,1,0:T(8,128)(2,1)}), bf16[1,320,2048]{2,1,0:T(8,128)(2,1)}) %all-gather.33.cloned.1.call-update) | async-done | bytes 1310736 | tf_op jit(solution)/shard_map/all_gather | solution.py:110
  119.6 24.2 %all-gather.21.cloned.1.call-done = bf16[2048,640]{1,0:T(8,128)(2,1)} async-done(((bf16[256,640]{1,0:T(8,128)(2,1)}), bf16[2048,640]{1,0:T(8,128)(2,1)}) %all-gather.21.cloned.1.call-update) | async-done | bytes 2621456 | tf_op jit(solution)/shard_map/all_gather | solution.py:100
  479.3 51.8 %reduce-scatter.19.cloned.1.call-done = f32[1,80,2048]{2,1,0:T(8,128)} async-done(((f32[1,320,2048]{2,1,0:T(8,128)}), f32[1,80,2048]{2,1,0:T(8,128)}) %reduce-scatter.19.cloned.1.call-update) | async-done | bytes 655376 | tf_op jit(solution)/shard_map/reduce_scatter | solution.py:114
  537.4 40.8 %all-gather.27.cloned.1.call-done = bf16[2048,1536]{1,0:T(8,128)(2,1)} async-done(((bf16[256,1536]{1,0:T(8,128)(2,1)}), bf16[2048,1536]{1,0:T(8,128)(2,1)}) %all-gather.27.cloned.1.call-update) | async-done | bytes 6291472 | tf_op jit(solution)/shard_map/all_gather | solution.py:102
  578.2 34.9 %all-gather.25.cloned.1.call-done = bf16[1,320,2048]{2,1,0:T(8,128)(2,1)} async-done(((bf16[1,80,2048]{2,1,0:T(8,128)(2,1)}), bf16[1,320,2048]{2,1,0:T(8,128)(2,1)}) %all-gather.25.cloned.1.call-update) | async-done | bytes 1310736 | tf_op jit(solution)/shard_map/all_gather | solution.py:110
  613.1 6.7 fusion.51
  619.8 39.6 %all-gather.29.cloned.1.call-done = bf16[2048,1536]{1,0:T(8,128)(2,1)} async-done(((bf16[256,1536]{1,0:T(8,128)(2,1)}), bf16[2048,1536]{1,0:T(8,128)(2,1)}) %all-gather.29.cloned.1.call-update) | async-done | bytes 6291472 | tf_op jit(solution)/shard_map/all_gather | solution.py:103
  659.4 6.7 fusion.49
  666.0 28.2 %all-gather.41.cloned.1.call-done = bf16[1,1,320,2048]{3,2,1,0:T(8,128)(2,1)} async-done(((bf16[1,1,80,2048]{3,2,1,0:T(8,128)(2,1)}), bf16[1,1,320,2048]{3,2,1,0:T(8,128)(2,1)}) %all-gather.41.cloned.1.call-update) | async-done | bytes 1310736 | tf_op jit(solution)/shard_map/all_gather | solution.py:118
  694.2 47.4 %all-gather.31.cloned.1.call-done = bf16[1536,2048]{1,0:T(8,128)(2,1)} async-done(((bf16[1536,256]{1,0:T(8,128)(2,1)}), bf16[1536,2048]{1,0:T(8,128)(2,1)}) %all-gather.31.cloned.1.call-update) | async-done | bytes 6291472 | tf_op jit(solution)/shard_map/all_gather | solution.py:105
  741.7 9.0 multiply_convert_fusion.1
  750.6 5.8 fusion.252
  760.5 52.0 %reduce-scatter.23.cloned.1.call-done = f32[1,80,2048]{2,1,0:T(8,128)} async-done(((f32[1,320,2048]{2,1,0:T(8,128)}), f32[1,80,2048]{2,1,0:T(8,128)}) %reduce-scatter.23.cloned.1.call-update) | async-done | bytes 655376 | tf_op jit(solution)/shard_map/reduce_scatter | solution.py:122
  817.8 31.9 %all-gather.35.cloned.1.call-done = bf16[1,320,2048]{2,1,0:T(8,128)(2,1)} async-done(((bf16[1,80,2048]{2,1,0:T(8,128)(2,1)}), bf16[1,320,2048]{2,1,0:T(8,128)(2,1)}) %all-gather.35.cloned.1.call-update) | async-done | bytes 1310736 | tf_op jit(solution)/shard_map/all_gather | solution.py:110
  849.6 6.8 fusion.36
  856.4 6.5 fusion.34
  863.0 20.4 all-gather.43.cloned.1.call-done
  883.4 8.9 multiply_convert_fusion
  892.2 5.7 fusion.253
  897.9 6.5 fusion.2
  904.6 6.9 convolution_bitcast_fusion
  911.5 44.2 %reduce-scatter.27.cloned.1.call-done = f32[1,80,2048]{2,1,0:T(8,128)} async-done(((f32[1,320,2048]{2,1,0:T(8,128)}), f32[1,80,2048]{2,1,0:T(8,128)}) %reduce-scatter.27.cloned.1.call-update) | async-done | bytes 655376 | tf_op jit(solution)/shard_map/reduce_scatter | solution.py:122
  959.5 50.2 %reduce-scatter.21.cloned.1.call-done = f32[1,80,2048]{2,1,0:T(8,128)} async-done(((f32[1,320,2048]{2,1,0:T(8,128)}), f32[1,80,2048]{2,1,0:T(8,128)}) %reduce-scatter.21.cloned.1.call-update) | async-done | bytes 655376 | tf_op jit(solution)/shard_map/reduce_scatter | solution.py:114
  1036.5 5.7 slice.1250
  1053.5 5.7 slice.1334
  1064.8 5.6 slice.1336
  1088.6 5.6 slice.1254
  1343.9 5.7 slice.1311
  1443.5 5.7 slice.1395
  1490.2 9.6 fusion.47
  1504.4 8.2 rev.17
  1512.6 8.1 rev.18
  1520.7 8.2 rev.19
  1528.9 8.1 rev.20
  1557.7 11.4 add_convert_fusion.2
  1660.1 6.6 convolution_bitcast_fusion.1
  1667.6 28.4 %all-reduce.153 = (bf16[4,640]{1,0:T(4,128)(2,1)S(1)}, bf16[640]{0:T(1024)(128)(2,1)S(1)}, bf16[640]{0:T(1024)(128)(2,1)S(1)}, bf16[640]{0:T(1024)(128)(2,1)S(1)}, bf16[640]{0:T(1024)(128)(2,1)S(1)}) all-reduce(bf16[4,640]{1,0:T(4,128)(2,1)S(1)} %add_convert_fusion.10, ...), channel_id=1, replica_groups=mesh['fsdp'=2,'context'=4,'tensor'=4] {'fsdp','context'}, use_global_device_ids=true, to_apply=%region_29.31 | all-reduce | flops 5120 | bytes 20480 | tf_op jit(solution)/shard_map/psum | solution.py:307
  1705.2 40.2 %reduce-scatter.39.cloned.1.call-done = bf16[256,1536]{1,0:T(8,128)(2,1)} async-done(((bf16[2048,1536]{1,0:T(8,128)(2,1)}), bf16[256,1536]{1,0:T(8,128)(2,1)}) %reduce-scatter.39.cloned.1.call-update) | async-done | bytes 786448 | tf_op jit(solution)/shard_map/reduce_scatter | solution.py:296
  1747.9 63.1 %reduce-scatter.41.cloned.1.call-done = bf16[1536,256]{1,0:T(8,128)(2,1)} async-done(((bf16[1536,2048]{1,0:T(8,128)(2,1)}), bf16[1536,256]{1,0:T(8,128)(2,1)}) %reduce-scatter.41.cloned.1.call-update) | async-done | bytes 786448 | tf_op jit(solution)/shard_map/reduce_scatter | solution.py:302
  1813.3 44.5 %reduce-scatter.31.cloned.1.call-done = bf16[256,640]{1,0:T(8,128)(2,1)} async-done(((bf16[2048,640]{1,0:T(8,128)(2,1)}), bf16[256,640]{1,0:T(8,128)(2,1)}) %reduce-scatter.31.cloned.1.call-update) | async-done | bytes 327696 | tf_op jit(solution)/shard_map/reduce_scatter | solution.py:287
  1859.7 45.1 %reduce-scatter.35.cloned.1.call-done = bf16[640,256]{1,0:T(8,128)(2,1)} async-done(((bf16[640,2048]{1,0:T(8,128)(2,1)}), bf16[640,256]{1,0:T(8,128)(2,1)}) %reduce-scatter.35.cloned.1.call-update) | async-done | bytes 327696 | tf_op jit(solution)/shard_map/reduce_scatter | solution.py:299
  1906.7 45.0 %reduce-scatter.33.cloned.1.call-done = bf16[256,640]{1,0:T(8,128)(2,1)} async-done(((bf16[2048,640]{1,0:T(8,128)(2,1)}), bf16[256,640]{1,0:T(8,128)(2,1)}) %reduce-scatter.33.cloned.1.call-update) | async-done | bytes 327696 | tf_op jit(solution)/shard_map/reduce_scatter | solution.py:290
  1953.5 52.4 %reduce-scatter.25.cloned.1.call-done = f32[1,80,2048]{2,1,0:T(8,128)} async-done(((f32[1,320,2048]{2,1,0:T(8,128)}), f32[1,80,2048]{2,1,0:T(8,128)}) %reduce-scatter.25.cloned.1.call-update) | async-done | bytes 655376 | tf_op jit(solution)/shard_map/reduce_scatter | solution.py:122
  2007.8 52.2 %reduce-scatter.29.cloned.1.call-done = f32[1,80,2048]{2,1,0:T(8,128)} async-done(((f32[1,320,2048]{2,1,0:T(8,128)}), f32[1,80,2048]{2,1,0:T(8,128)}) %reduce-scatter.29.cloned.1.call-update) | async-done | bytes 655376 | tf_op jit(solution)/shard_map/reduce_scatter | solution.py:122
  2065.1 49.0 %reduce-scatter.17.cloned.1.call-done = f32[1,80,2048]{2,1,0:T(8,128)} async-done(((f32[1,320,2048]{2,1,0:T(8,128)}), f32[1,80,2048]{2,1,0:T(8,128)}) %reduce-scatter.17.cloned.1.call-update) | async-done | bytes 655376 | tf_op jit(solution)/shard_map/reduce_scatter | solution.py:114
  2118.0 40.0 %all-reduce.152 = (f32[2048]{0:T(1024)}, f32[2048]{0:T(1024)}) all-reduce(f32[2048]{0:T(1024)S(1)} %add.1474, f32[2048]{0:T(1024)S(1)} %add.1485), channel_id=1, replica_groups=mesh['fsdp'=2,'context'=4,'tensor'=4] {'fsdp','context','tensor'}, use_global_device_ids=true, to_apply=%region_18.20 | all-reduce | flops 4096 | bytes 32768 | tf_op jit(solution)/shard_map/psum | solution.py:315
  (1199 shorter events, 966.8 us)
Async XLA Ops:
  7.2 39.7 %all-gather.17.cloned.1.call-start = ((), (), s32[]{:S(2)}) async-start(), calls=%async_computation.14 | async-start | bytes 1638400 | tf_op jit(solution)/shard_map/all_gather | solution.py:110
  11.4 66.6 %all-gather.19.cloned.1.call-start = ((), (), s32[]{:S(2)}) async-start(), calls=%async_computation.15 | async-start | bytes 2949120 | tf_op jit(solution)/shard_map/all_gather | solution.py:101
  12.1 100.7 %all-gather.33.cloned.1.call-start = ((), (), s32[]{:S(2)}) async-start(), calls=%async_computation.24 | async-start | bytes 1638400 | tf_op jit(solution)/shard_map/all_gather | solution.py:110
  12.9 130.8 %all-gather.21.cloned.1.call-start = ((), (), s32[]{:S(2)}) async-start(), calls=%async_computation.16 | async-start | bytes 2949120 | tf_op jit(solution)/shard_map/all_gather | solution.py:100
  13.5 391.9 %all-gather.23.cloned.1.call-start = ((), (), s32[]{:S(2)}) async-start(), calls=%async_computation.17 | async-start | bytes 2949120 | tf_op jit(solution)/shard_map/all_gather | solution.py:104
  14.0 465.2 %reduce-scatter.15.cloned.1.call-start = ((), (), s32[]{:S(2)}) async-start(), calls=%async_computation.18 | async-start | bytes 3276800 | tf_op jit(solution)/shard_map/reduce_scatter | solution.py:114
  81.3 66.2 %collective-permute-start = (bf16[1,3,640]{2,1,0:T(4,128)(2,1)S(1)}, bf16[1,3,640]{2,1,0:T(4,128)(2,1)S(1)}, u32[]{:S(2)}, u32[]{:S(2)}) collective-permute-start(bf16[1,3,640]{2,1,0:T(4,128)(2,1)S(1)} %slice.1414), channel_id=1, source_target_pairs={{0,4},{4,8},{8,12},{1,5},{5,9},{9,13},{2,6},{6,10},{10,14},{3,7},{... | collective-permute-start | bytes 11528 | tf_op jit(solution)/shard_map/ppermute | solution.py:15
  116.2 31.5 %collective-permute-start.4 = (bf16[1,3,640]{2,1,0:T(4,128)(2,1)S(1)}, bf16[1,3,640]{2,1,0:T(4,128)(2,1)S(1)}, u32[]{:S(2)}, u32[]{:S(2)}) collective-permute-start(bf16[1,3,640]{2,1,0:T(4,128)(2,1)S(1)} %slice.1465), channel_id=1, source_target_pairs={{0,4},{4,8},{8,12},{1,5},{5,9},{9,13},{2,6},{6,10},{10,14},{3,7},{... | collective-permute-start | bytes 11528 | tf_op jit(solution)/shard_map/ppermute | solution.py:15
  156.9 1385.0 %copy-start.5 = (f32[1,320,640]{2,1,0:T(8,128)}, f32[1,320,640]{2,1,0:T(8,128)S(1)}, u32[]{:S(2)}) copy-start(f32[1,320,640]{2,1,0:T(8,128)S(1)} %copy.70) | copy-start | bytes 2457604
  340.7 8.9 collective-permute-start.1
  350.9 10.0 collective-permute-start.2
  362.2 39.7 %collective-permute-start.3 = (f32[1,640]{1,0:T(1,128)}, f32[1,640]{1,0:T(1,128)S(1)}, u32[]{:S(2)}, u32[]{:S(2)}) collective-permute-start(f32[1,640]{1,0:T(1,128)} %multiply_add_fusion.45), channel_id=1, source_target_pairs={{0,4},{4,8},{8,12},{1,5},{5,9},{9,13},{2,6},{6,10},{10,14},{3,7},{... | collective-permute-start | bytes 7688 | tf_op jit(solution)/shard_map/ppermute | solution.py:15
  410.2 120.9 %reduce-scatter.19.cloned.1.call-start = ((), (), s32[]{:S(2)}) async-start(), calls=%async_computation.25 | async-start | bytes 3276800 | tf_op jit(solution)/shard_map/reduce_scatter | solution.py:114
  452.6 3.2 collective-permute-start.5
  456.6 5.5 collective-permute-start.6
  462.8 8.6 collective-permute-start.7
  478.5 99.7 %all-gather.27.cloned.1.call-start = ((), (), s32[]{:S(2)}) async-start(), calls=%async_computation.20 | async-start | bytes 7077888 | tf_op jit(solution)/shard_map/all_gather | solution.py:102
  479.2 133.9 %all-gather.25.cloned.1.call-start = ((), (), s32[]{:S(2)}) async-start(), calls=%async_computation.19 | async-start | bytes 1638400 | tf_op jit(solution)/shard_map/all_gather | solution.py:110
  533.5 476.2 %copy-start.206 = (f32[80]{0:T(128)}, f32[80]{0:T(128)S(1)}, u32[]{:S(2)}) copy-start(f32[80]{0:T(128)S(1)} %fusion.194) | copy-start | bytes 964
  535.2 124.2 %all-gather.29.cloned.1.call-start = ((), (), s32[]{:S(2)}) async-start(), calls=%async_computation.21 | async-start | bytes 7077888 | tf_op jit(solution)/shard_map/all_gather | solution.py:103
  535.8 158.4 %all-gather.41.cloned.1.call-start = ((), (), s32[]{:S(2)}) async-start(), calls=%async_computation.40 | async-start | bytes 1638400 | tf_op jit(solution)/shard_map/all_gather | solution.py:118
  536.7 204.9 %all-gather.31.cloned.1.call-start = ((), (), s32[]{:S(2)}) async-start(), calls=%async_computation.22 | async-start | bytes 7077888 | tf_op jit(solution)/shard_map/all_gather | solution.py:105
  537.3 275.2 %reduce-scatter.23.cloned.1.call-start = ((), (), s32[]{:S(2)}) async-start(), calls=%async_computation.28 | async-start | bytes 3276800 | tf_op jit(solution)/shard_map/reduce_scatter | solution.py:122
  760.2 89.4 %all-gather.35.cloned.1.call-start = ((), (), s32[]{:S(2)}) async-start(), calls=%async_computation.26 | async-start | bytes 1638400 | tf_op jit(solution)/shard_map/all_gather | solution.py:110
  760.5 249.2 %copy-start.208 = (f32[80]{0:T(128)}, f32[80]{0:T(128)S(1)}, u32[]{:S(2)}) copy-start(f32[80]{0:T(128)S(1)} %fusion.196) | copy-start | bytes 964
  817.1 66.2 %all-gather.43.cloned.1.call-start = ((), (), s32[]{:S(2)}) async-start(), calls=%async_computation.41 | async-start | bytes 1638400 | tf_op jit(solution)/shard_map/all_gather | solution.py:118
  817.7 138.0 %reduce-scatter.27.cloned.1.call-start = ((), (), s32[]{:S(2)}) async-start(), calls=%async_computation.31 | async-start | bytes 3276800 | tf_op jit(solution)/shard_map/reduce_scatter | solution.py:122
  904.5 105.2 %reduce-scatter.21.cloned.1.call-start = ((), (), s32[]{:S(2)}) async-start(), calls=%async_computation.27 | async-start | bytes 3276800 | tf_op jit(solution)/shard_map/reduce_scatter | solution.py:114
  911.4 159.1 %all-gather.37.cloned.1.call-start = ((), (), s32[]{:S(2)}) async-start(), calls=%async_computation.29 | async-start | bytes 1638400 | tf_op jit(solution)/shard_map/all_gather | solution.py:118
  1012.8 161.6 %all-gather.39.cloned.1.call-start = ((), (), s32[]{:S(2)}) async-start(), calls=%async_computation.32 | async-start | bytes 1638400 | tf_op jit(solution)/shard_map/all_gather | solution.py:118
  1070.5 628.5 %all-reduce.157.cloned.1.call-start = ((), (), s32[]{:S(2)}) async-start(), calls=%async_computation.42 | async-start | bytes 1310720 | tf_op jit(solution)/shard_map/psum | solution.py:309
  1377.1 100.5 %collective-permute-start.8 = (f32[1,640]{1,0:T(1,128)}, f32[1,640]{1,0:T(1,128)}, u32[]{:S(2)}, u32[]{:S(2)}) collective-permute-start(f32[1,640]{1,0:T(1,128)} %get-tuple-element.78), channel_id=1, source_target_pairs={{4,0},{8,4},{12,8},{5,1},{9,5},{13,9},{6,2},{10,6},{14,10},{7,3},{... | collective-permute-start | bytes 7688 | tf_op jit(solution)/shard_map/ppermute | solution.py:15
  1476.2 6.1 collective-permute-start.12
  1478.2 6.7 collective-permute-start.9
  1482.3 6.4 collective-permute-start.13
  1485.0 52.0 %collective-permute-start.10 = (f32[1,640]{1,0:T(1,128)S(1)}, f32[1,640]{1,0:T(1,128)S(1)}, u32[]{:S(2)}, u32[]{:S(2)}) collective-permute-start(f32[1,640]{1,0:T(1,128)S(1)} %multiply_add_fusion.39), channel_id=1, source_target_pairs={{4,0},{8,4},{12,8},{5,1},{9,5},{13,9},{6,2},{10,6},{14,10},{7,3},{... | collective-permute-start | bytes 7688 | tf_op jit(solution)/shard_map/ppermute | solution.py:15
  1488.7 48.3 %collective-permute-start.14 = (f32[1,640]{1,0:T(1,128)S(1)}, f32[1,640]{1,0:T(1,128)S(1)}, u32[]{:S(2)}, u32[]{:S(2)}) collective-permute-start(f32[1,640]{1,0:T(1,128)S(1)} %multiply_add_fusion.36), channel_id=1, source_target_pairs={{4,0},{8,4},{12,8},{5,1},{9,5},{13,9},{6,2},{10,6},{14,10},{7,3},{... | collective-permute-start | bytes 7688 | tf_op jit(solution)/shard_map/ppermute | solution.py:15
  1557.5 145.3 %reduce-scatter.37.cloned.1.call-start = ((), (), s32[]{:S(2)}) async-start(), calls=%async_computation.37 | async-start | bytes 7077888 | tf_op jit(solution)/shard_map/reduce_scatter | solution.py:293
  1569.1 176.3 %reduce-scatter.39.cloned.1.call-start = ((), (), s32[]{:S(2)}) async-start(), calls=%async_computation.38 | async-start | bytes 7077888 | tf_op jit(solution)/shard_map/reduce_scatter | solution.py:296
  1580.1 230.9 %reduce-scatter.41.cloned.1.call-start = ((), (), s32[]{:S(2)}) async-start(), calls=%async_computation.39 | async-start | bytes 7077888 | tf_op jit(solution)/shard_map/reduce_scatter | solution.py:302
  1591.4 266.4 %reduce-scatter.31.cloned.1.call-start = ((), (), s32[]{:S(2)}) async-start(), calls=%async_computation.34 | async-start | bytes 2949120 | tf_op jit(solution)/shard_map/reduce_scatter | solution.py:287
  1598.9 305.9 %reduce-scatter.35.cloned.1.call-start = ((), (), s32[]{:S(2)}) async-start(), calls=%async_computation.36 | async-start | bytes 2949120 | tf_op jit(solution)/shard_map/reduce_scatter | solution.py:299
  1606.0 345.6 %reduce-scatter.33.cloned.1.call-start = ((), (), s32[]{:S(2)}) async-start(), calls=%async_computation.35 | async-start | bytes 2949120 | tf_op jit(solution)/shard_map/reduce_scatter | solution.py:290
  1631.8 7.3 collective-permute-start.15
  1633.7 8.2 collective-permute-start.11
  1645.1 360.8 %reduce-scatter.25.cloned.1.call-start = ((), (), s32[]{:S(2)}) async-start(), calls=%async_computation.30 | async-start | bytes 3276800 | tf_op jit(solution)/shard_map/reduce_scatter | solution.py:122
  1652.0 408.0 %reduce-scatter.29.cloned.1.call-start = ((), (), s32[]{:S(2)}) async-start(), calls=%async_computation.33 | async-start | bytes 3276800 | tf_op jit(solution)/shard_map/reduce_scatter | solution.py:122
  1658.9 455.2 %reduce-scatter.17.cloned.1.call-start = ((), (), s32[]{:S(2)}) async-start(), calls=%async_computation.23 | async-start | bytes 3276800 | tf_op jit(solution)/shard_map/reduce_scatter | solution.py:114
  (222 other events, 5514.9 us)
Sparse Core Ops, SparseCore 0:
  11.5 35.3 all-gather.16
  48.8 29.0 all-gather.18
  80.1 32.6 all-gather.32
  114.6 29.0 all-gather.20
  145.4 30.5 all-gather.22
  410.3 51.2 reduce-scatter.14
  478.6 52.4 reduce-scatter.18
  533.0 45.1 all-gather.26
  580.3 32.6 all-gather.24
  614.8 44.5 all-gather.28
  661.5 32.6 all-gather.40
  696.0 45.6 all-gather.30
  760.4 52.1 reduce-scatter.22
  817.2 32.3 all-gather.34
  851.6 31.6 all-gather.42
  904.6 51.0 reduce-scatter.26
  957.9 51.7 reduce-scatter.20
  1012.9 32.3 all-gather.36
  1070.6 32.3 all-gather.38
  1557.6 57.4 all-reduce.156
  1618.8 61.1 reduce-scatter.36
  1683.5 61.9 reduce-scatter.38
  1749.2 61.7 reduce-scatter.40
  1814.1 43.6 reduce-scatter.30
  1861.1 43.6 reduce-scatter.34
  1908.0 43.6 reduce-scatter.32
  1953.8 52.0 reduce-scatter.24
  2008.2 51.7 reduce-scatter.28
  2062.3 51.7 reduce-scatter.16
where the time goes:
time: 2200 us; the launch traced here: 2160 us
  waiting for transfers between devices  968 us (44%)
  local copies, waits for them, and re-layouts  614 us (28%)
  other arithmetic  256 us (12%)
  matrix products  200 us (9%)
  blocking collectives  68.4 us (3%)
  starting transfers between devices  40.2 us (2%)
    slice x234, local copies, waits for them, and re-layouts, local_scan(): return lax.associative_scan(combine, (coeffs, offsets), axis=1)  388 us
    reduce_scatter x4, waiting for transfers between devices, narrow_grads(): lax.psum_scatter(partial_vals, 'tensor', scatter_dimension=1, tiled=True)  201 us
    reduce_scatter x4, waiting for transfers between devices, narrow_rows(): lax.psum_scatter(partial_vals, 'tensor', scatter_dimension=1, tiled=True)  151 us
    pad x112, local copies, waits for them, and re-layouts, local_scan(): return lax.associative_scan(combine, (coeffs, offsets), axis=1)  149 us
    all_gather x4, waiting for transfers between devices, widen_rows(): return lax.all_gather(values, 'tensor', axis=1, tiled=True)  127 us
    mul x56, other arithmetic, combine(): return (earlier[0] * following[0], following[0] * earlier[1] + following[1])  76.4 us
    reduce_scatter x1, waiting for transfers between devices, per_device(): lax.psum_scatter(totals[14].astype(jnp.bfloat16), ('fsdp', 'context'), sc...  63.1 us
    dot_general x12, matrix products, project(): jnp.einsum('sla,ab->slb', rows_in, weight, preferred_element_type=jnp.flo...  62.1 us
  transfers between devices with their start and end apart: 45, of which 30 were waited for; matrix products, arithmetic and copies ran while one was open for 36% of the time, Pallas kernels for 0%

commit v1 on v0

--- a/solution.py
+++ b/solution.py
@@ -7,6 +7,25 @@
 CONV = 4
 CPOW = 8
 EPS = 1e-06
+
+
+def collect(x, axis, dim):
+    size, here, span = (lax.axis_size(axis), lax.axis_index(axis), x.shape[dim])
+    forward = [(i, (i + 1) % size) for i in range(size)]
+    backward = [(i, (i - 1) % size) for i in range(size)]
+    out = jnp.zeros((*x.shape[:dim], size * span, *x.shape[dim + 1 :]), x.dtype)
+    out = lax.dynamic_update_slice_in_dim(out, x, here * span, axis=dim)
+    from_left = from_right = x
+    half = size // 2
+    for step in range(1, half + 1):
+        from_left = lax.ppermute(from_left, axis, forward)
+        out = lax.dynamic_update_slice_in_dim(out, from_left, (here - step) % size * span, axis=dim)
+        if step < size - half:
+            from_right = lax.ppermute(from_right, axis, backward)
+            out = lax.dynamic_update_slice_in_dim(
+                out, from_right, (here + step) % size * span, axis=dim
+            )
+    return out
 
 
 def from_behind(value, axis, by):
@@ -107,7 +126,7 @@
 
 
 def widen_rows(values):
-    return lax.all_gather(values, "tensor", axis=1, tiled=True)
+    return collect(values, "tensor", 1)
 
 
 def narrow_rows(partial_vals):

time: 2200 us -> 2060 us (0.936)
  waiting for transfers between devices: 968 us -> 795 us
  starting transfers between devices: 40.2 us -> 76.5 us
    all_gather x4 -> x0, waiting for transfers between devices: 127 us -> none  [widen_rows(): return lax.all_gather(values, 'tensor', axis=1, tiled=True)]
    ppermute x0 -> x12, waiting for transfers between devices: none -> 85.1 us  [the longest x8 50.1 us: collect(): from_left = lax.ppermute(from_left, axis, forward)]
    all_gather x4, waiting for transfers between devices: 48.6 us -> 0.02 us  [widen_grads(): return lax.all_gather(values, 'tensor', axis=1, tiled=True)]
    ppermute x0 -> x12, starting transfers between devices: none -> 36.7 us  [the longest x8 24.2 us: collect(): from_left = lax.ppermute(from_left, axis, forward)]
    all_gather x1, waiting for transfers between devices: 31 us -> 0.02 us  [fetch_weights(): lax.all_gather(inner_w, ('fsdp', 'context'), axis=0, tiled=True)]
    reduce_scatter x4, waiting for transfers between devices: 201 us -> 179 us  [narrow_grads(): lax.psum_scatter(partial_vals, 'tensor', scatter_dimension=1, tiled=True)]
  transfers between devices with their start and end apart: 45 -> 53, of which waited for: 30 -> 32; matrix products, arithmetic and copies ran while one was open for 36% -> 44% of each run, Pallas kernels for 0% -> 0%
where the time goes in v1:
time: 2060 us; the launch traced here: 2030 us
  waiting for transfers between devices  795 us (39%)
  local copies, waits for them, and re-layouts  627 us (30%)
  other arithmetic  262 us (13%)
  matrix products  184 us (9%)
  starting transfers between devices  76.5 us (4%)
  blocking collectives  68.4 us (3%)
    slice x234, local copies, waits for them, and re-layouts, local_scan(): return lax.associative_scan(combine, (coeffs, offsets), axis=1)  386 us
    reduce_scatter x4, waiting for transfers between devices, narrow_grads(): lax.psum_scatter(partial_vals, 'tensor', scatter_dimension=1, tiled=True)  179 us
    pad x112, local copies, waits for them, and re-layouts, local_scan(): return lax.associative_scan(combine, (coeffs, offsets), axis=1)  158 us
    reduce_scatter x4, waiting for transfers between devices, narrow_rows(): lax.psum_scatter(partial_vals, 'tensor', scatter_dimension=1, tiled=True)  147 us
    mul x56, other arithmetic, combine(): return (earlier[0] * following[0], following[0] * earlier[1] + following[1])  76.1 us
    reduce_scatter x1, waiting for transfers between devices, per_device(): lax.psum_scatter(totals[14].astype(jnp.bfloat16), ('fsdp', 'context'), sc...  63.1 us
    dot_general x12, matrix products, project(): jnp.einsum('sla,ab->slb', rows_in, weight, preferred_element_type=jnp.flo...  60.9 us
    dot_general x12, matrix products, outer_sum(): jnp.einsum('sla,slb->ab', rows_in, grad_vals, preferred_element_type=jnp....  60.9 us
  transfers between devices with their start and end apart: 53, of which 32 were waited for; matrix products, arithmetic and copies ran while one was open for 44% of the time, Pallas kernels for 0%

profile of v1, /device:TPU:0, one launch (start us, length us, event | category | flops | bytes accessed | tf_op | source)
XLA Modules:
  0.0 2030.8 jit_solution(13684410850203303944)
XLA Ops:
  26.2 5.8 collective-permute-start.2
  31.9 8.3 collective-permute-done.10
  40.3 5.7 collective-permute-start.12
  48.5 5.8 collective-permute-done.2
  570.7 47.8 %reduce-scatter.19.cloned.1.call-done = f32[1,80,2048]{2,1,0:T(8,128)} async-done(((f32[1,320,2048]{2,1,0:T(8,128)}), f32[1,80,2048]{2,1,0:T(8,128)}) %reduce-scatter.19.cloned.1.call-update) | async-done | bytes 655376 | tf_op jit(solution)/shard_map/reduce_scatter | solution.py:133
  628.4 8.8 collective-permute-done.7
  637.2 8.9 collective-permute-start.9
  646.8 10.7 collective-permute-done.8
  658.3 17.4 collective-permute-done.9
  676.4 45.1 %all-gather.23.cloned.1.call-done = bf16[1536,2048]{1,0:T(8,128)(2,1)} async-done(((bf16[1536,256]{1,0:T(8,128)(2,1)}), bf16[1536,2048]{1,0:T(8,128)(2,1)}) %all-gather.23.cloned.1.call-update) | async-done | bytes 6291472 | tf_op jit(solution)/shard_map/all_gather | solution.py:124
  721.5 6.7 fusion.30
  728.2 40.7 %all-gather.21.cloned.1.call-done = bf16[2048,1536]{1,0:T(8,128)(2,1)} async-done(((bf16[256,1536]{1,0:T(8,128)(2,1)}), bf16[2048,1536]{1,0:T(8,128)(2,1)}) %all-gather.21.cloned.1.call-update) | async-done | bytes 6291472 | tf_op jit(solution)/shard_map/all_gather | solution.py:122
  769.0 6.7 fusion.235
  775.6 40.8 %all-gather.19.cloned.1.call-done = bf16[2048,1536]{1,0:T(8,128)(2,1)} async-done(((bf16[256,1536]{1,0:T(8,128)(2,1)}), bf16[2048,1536]{1,0:T(8,128)(2,1)}) %all-gather.19.cloned.1.call-update) | async-done | bytes 6291472 | tf_op jit(solution)/shard_map/all_gather | solution.py:121
  816.4 8.9 multiply_convert_fusion.1
  837.0 24.3 %collective-permute-done.18 = bf16[1,80,2048]{2,1,0:T(8,128)(2,1)S(1)} collective-permute-done((bf16[1,80,2048]{2,1,0:T(8,128)(2,1)}, bf16[1,80,2048]{2,1,0:T(8,128)(2,1)S(1)}, u32[]{:S(2)}, u32[]{:S(2)}) %collective-permute-start.18) | collective-permute-done | bytes 327712 | tf_op jit(solution)/shard_map/ppermute | solution.py:24
  872.0 5.7 fusion.239
  877.8 6.0 multiply_convert_fusion
  889.9 6.9 convolution_bitcast_fusion
  896.8 21.8 %reduce-scatter.23.cloned.1.call-done = f32[1,80,2048]{2,1,0:T(8,128)} async-done(((f32[1,320,2048]{2,1,0:T(8,128)}), f32[1,80,2048]{2,1,0:T(8,128)}) %reduce-scatter.23.cloned.1.call-update) | async-done | bytes 655376 | tf_op jit(solution)/shard_map/reduce_scatter | solution.py:141
  920.5 52.1 %reduce-scatter.27.cloned.1.call-done = f32[1,80,2048]{2,1,0:T(8,128)} async-done(((f32[1,320,2048]{2,1,0:T(8,128)}), f32[1,80,2048]{2,1,0:T(8,128)}) %reduce-scatter.27.cloned.1.call-update) | async-done | bytes 655376 | tf_op jit(solution)/shard_map/reduce_scatter | solution.py:141
  976.5 50.3 %reduce-scatter.21.cloned.1.call-done = f32[1,80,2048]{2,1,0:T(8,128)} async-done(((f32[1,320,2048]{2,1,0:T(8,128)}), f32[1,80,2048]{2,1,0:T(8,128)}) %reduce-scatter.21.cloned.1.call-update) | async-done | bytes 655376 | tf_op jit(solution)/shard_map/reduce_scatter | solution.py:133
  1040.0 5.7 slice.1250
  1045.7 5.6 slice.1259
  1051.3 5.7 slice.1252
  1057.0 5.7 slice.1334
  1068.3 5.6 slice.1336
  1082.0 5.6 slice.1256
  1087.6 5.6 slice.1254
  1175.3 5.6 slice.1340
  1276.3 5.7 slice.1311
  1322.0 5.7 slice.1395
  1364.6 9.5 fusion.244
  1388.9 8.2 rev.19
  1397.1 8.1 rev.20
  1424.0 11.4 add_convert_fusion.2
  1441.5 7.1 add_convert_fusion.1
  1527.5 6.6 convolution_bitcast_fusion.1
  1535.0 28.3 %all-reduce.153 = (bf16[4,640]{1,0:T(4,128)(2,1)S(1)}, bf16[640]{0:T(1024)(128)(2,1)S(1)}, bf16[640]{0:T(1024)(128)(2,1)S(1)}, bf16[640]{0:T(1024)(128)(2,1)S(1)}, bf16[640]{0:T(1024)(128)(2,1)S(1)}) all-reduce(bf16[4,640]{1,0:T(4,128)(2,1)S(1)} %add_convert_fusion.10, ...), channel_id=1, replica_groups=mesh['fsdp'=2,'context'=4,'tensor'=4] {'fsdp','context'}, use_global_device_ids=true, to_apply=%region_29.31 | all-reduce | flops 5120 | bytes 20480 | tf_op jit(solution)/shard_map/psum | solution.py:326
  1572.5 38.8 %reduce-scatter.39.cloned.1.call-done = bf16[256,1536]{1,0:T(8,128)(2,1)} async-done(((bf16[2048,1536]{1,0:T(8,128)(2,1)}), bf16[256,1536]{1,0:T(8,128)(2,1)}) %reduce-scatter.39.cloned.1.call-update) | async-done | bytes 786448 | tf_op jit(solution)/shard_map/reduce_scatter | solution.py:315
  1613.8 63.1 %reduce-scatter.41.cloned.1.call-done = bf16[1536,256]{1,0:T(8,128)(2,1)} async-done(((bf16[1536,2048]{1,0:T(8,128)(2,1)}), bf16[1536,256]{1,0:T(8,128)(2,1)}) %reduce-scatter.41.cloned.1.call-update) | async-done | bytes 786448 | tf_op jit(solution)/shard_map/reduce_scatter | solution.py:321
  1679.3 44.5 %reduce-scatter.31.cloned.1.call-done = bf16[256,640]{1,0:T(8,128)(2,1)} async-done(((bf16[2048,640]{1,0:T(8,128)(2,1)}), bf16[256,640]{1,0:T(8,128)(2,1)}) %reduce-scatter.31.cloned.1.call-update) | async-done | bytes 327696 | tf_op jit(solution)/shard_map/reduce_scatter | solution.py:306
  1725.6 45.1 %reduce-scatter.35.cloned.1.call-done = bf16[640,256]{1,0:T(8,128)(2,1)} async-done(((bf16[640,2048]{1,0:T(8,128)(2,1)}), bf16[640,256]{1,0:T(8,128)(2,1)}) %reduce-scatter.35.cloned.1.call-update) | async-done | bytes 327696 | tf_op jit(solution)/shard_map/reduce_scatter | solution.py:318
  1772.6 45.1 %reduce-scatter.33.cloned.1.call-done = bf16[256,640]{1,0:T(8,128)(2,1)} async-done(((bf16[2048,640]{1,0:T(8,128)(2,1)}), bf16[256,640]{1,0:T(8,128)(2,1)}) %reduce-scatter.33.cloned.1.call-update) | async-done | bytes 327696 | tf_op jit(solution)/shard_map/reduce_scatter | solution.py:309
  1819.5 52.6 %reduce-scatter.25.cloned.1.call-done = f32[1,80,2048]{2,1,0:T(8,128)} async-done(((f32[1,320,2048]{2,1,0:T(8,128)}), f32[1,80,2048]{2,1,0:T(8,128)}) %reduce-scatter.25.cloned.1.call-update) | async-done | bytes 655376 | tf_op jit(solution)/shard_map/reduce_scatter | solution.py:141
  1874.0 52.1 %reduce-scatter.29.cloned.1.call-done = f32[1,80,2048]{2,1,0:T(8,128)} async-done(((f32[1,320,2048]{2,1,0:T(8,128)}), f32[1,80,2048]{2,1,0:T(8,128)}) %reduce-scatter.29.cloned.1.call-update) | async-done | bytes 655376 | tf_op jit(solution)/shard_map/reduce_scatter | solution.py:141
  1931.3 49.0 %reduce-scatter.17.cloned.1.call-done = f32[1,80,2048]{2,1,0:T(8,128)} async-done(((f32[1,320,2048]{2,1,0:T(8,128)}), f32[1,80,2048]{2,1,0:T(8,128)}) %reduce-scatter.17.cloned.1.call-update) | async-done | bytes 655376 | tf_op jit(solution)/shard_map/reduce_scatter | solution.py:133
  1984.1 40.0 %all-reduce.152 = (f32[2048]{0:T(1024)}, f32[2048]{0:T(1024)}) all-reduce(f32[2048]{0:T(1024)S(1)} %add.1533, f32[2048]{0:T(1024)S(1)} %add.1544), channel_id=1, replica_groups=mesh['fsdp'=2,'context'=4,'tensor'=4] {'fsdp','context','tensor'}, use_global_device_ids=true, to_apply=%region_18.20 | all-reduce | flops 4096 | bytes 32768 | tf_op jit(solution)/shard_map/psum | solution.py:334
  (1177 shorter events, 1011.9 us)
Async XLA Ops:
  7.2 53.3 %all-gather.13.cloned.1.call-start = ((), (), s32[]{:S(2)}) async-start(), calls=%async_computation.14 | async-start | bytes 2949120 | tf_op jit(solution)/shard_map/all_gather | solution.py:120
  7.9 66.9 %all-gather.15.cloned.1.call-start = ((), (), s32[]{:S(2)}) async-start(), calls=%async_computation.15 | async-start | bytes 2949120 | tf_op jit(solution)/shard_map/all_gather | solution.py:119
  8.7 419.3 %all-gather.17.cloned.1.call-start = ((), (), s32[]{:S(2)}) async-start(), calls=%async_computation.16 | async-start | bytes 2949120 | tf_op jit(solution)/shard_map/all_gather | solution.py:123
  12.3 13.8 collective-permute-start
  15.3 31.4 %collective-permute-start.1 = (bf16[1,80,2048]{2,1,0:T(8,128)(2,1)}, bf16[1,80,2048]{2,1,0:T(8,128)(2,1)S(1)}, u32[]{:S(2)}, u32[]{:S(2)}) collective-permute-start(bf16[1,80,2048]{2,1,0:T(8,128)(2,1)} %get-tuple-element.124), channel_id=1, source_target_pairs={{0,3},{1,0},{2,1},{3,2},{4,7},{5,4},{6,5},{7,6},{8,11},{9,8},{10,9... | collective-permute-start | bytes 983048 | tf_op jit(solution)/shard_map/ppermute | solution.py:24
  17.4 22.9 %collective-permute-start.10 = (bf16[1,80,2048]{2,1,0:T(8,128)(2,1)}, bf16[1,80,2048]{2,1,0:T(8,128)(2,1)S(1)}, u32[]{:S(2)}, u32[]{:S(2)}) collective-permute-start(bf16[1,80,2048]{2,1,0:T(8,128)(2,1)} %get-tuple-element.125), channel_id=1, source_target_pairs={{0,1},{1,2},{2,3},{3,0},{4,5},{5,6},{6,7},{7,4},{8,9},{9,10},{10,1... | collective-permute-start | bytes 983048 | tf_op jit(solution)/shard_map/ppermute | solution.py:21
  17.4 30.1 %collective-permute-start.11 = (bf16[1,80,2048]{2,1,0:T(8,128)(2,1)}, bf16[1,80,2048]{2,1,0:T(8,128)(2,1)}, u32[]{:S(2)}, u32[]{:S(2)}) collective-permute-start(bf16[1,80,2048]{2,1,0:T(8,128)(2,1)} %get-tuple-element.125), channel_id=1, source_target_pairs={{0,3},{1,0},{2,1},{3,2},{4,7},{5,4},{6,5},{7,6},{8,11},{9,8},{10,9... | collective-permute-start | bytes 983048 | tf_op jit(solution)/shard_map/ppermute | solution.py:24
  21.2 549.5 %reduce-scatter.15.cloned.1.call-start = ((), (), s32[]{:S(2)}) async-start(), calls=%async_computation.17 | async-start | bytes 3276800 | tf_op jit(solution)/shard_map/reduce_scatter | solution.py:133
  26.2 28.1 %collective-permute-start.2 = (bf16[1,80,2048]{2,1,0:T(8,128)(2,1)S(1)}, bf16[1,80,2048]{2,1,0:T(8,128)(2,1)S(1)}, u32[]{:S(2)}, u32[]{:S(2)}) collective-permute-start(bf16[1,80,2048]{2,1,0:T(8,128)(2,1)S(1)} %collective-permute-done), channel_id=1, source_target_pairs={{0,1},{1,2},{2,3},{3,0},{4,5},{5,6},{6,7},{7,4},{8,9},{9,10},{10,1... | collective-permute-start | bytes 983048 | tf_op jit(solution)/shard_map/ppermute | solution.py:21
  40.3 20.2 collective-permute-start.12
  64.4 14.7 collective-permute-start.3
  69.0 10.2 collective-permute-start.13
  357.1 9.7 collective-permute-start.4
  368.2 8.9 collective-permute-start.5
  377.8 46.0 %collective-permute-start.6 = (f32[1,640]{1,0:T(1,128)S(1)}, f32[1,640]{1,0:T(1,128)}, u32[]{:S(2)}, u32[]{:S(2)}) collective-permute-start(f32[1,640]{1,0:T(1,128)S(1)} %multiply_add_fusion.45), channel_id=1, source_target_pairs={{0,4},{4,8},{8,12},{1,5},{5,9},{9,13},{2,6},{6,10},{10,14},{3,7},{... | collective-permute-start | bytes 7688 | tf_op jit(solution)/shard_map/ppermute | solution.py:34
  432.6 185.9 %reduce-scatter.19.cloned.1.call-start = ((), (), s32[]{:S(2)}) async-start(), calls=%async_computation.22 | async-start | bytes 3276800 | tf_op jit(solution)/shard_map/reduce_scatter | solution.py:133
  550.6 8.2 collective-permute-start.16
  565.9 110.5 %all-gather.29.cloned.1.call-start = ((), (), s32[]{:S(2)}) async-start(), calls=%async_computation.36 | async-start | bytes 1638400 | tf_op jit(solution)/shard_map/all_gather | solution.py:137
  567.8 153.7 %all-gather.23.cloned.1.call-start = ((), (), s32[]{:S(2)}) async-start(), calls=%async_computation.20 | async-start | bytes 7077888 | tf_op jit(solution)/shard_map/all_gather | solution.py:124
  568.6 200.4 %all-gather.21.cloned.1.call-start = ((), (), s32[]{:S(2)}) async-start(), calls=%async_computation.19 | async-start | bytes 7077888 | tf_op jit(solution)/shard_map/all_gather | solution.py:122
  569.3 247.1 %all-gather.19.cloned.1.call-start = ((), (), s32[]{:S(2)}) async-start(), calls=%async_computation.18 | async-start | bytes 7077888 | tf_op jit(solution)/shard_map/all_gather | solution.py:121
  570.1 296.3 %all-gather.31.cloned.1.call-start = ((), (), s32[]{:S(2)}) async-start(), calls=%async_computation.37 | async-start | bytes 1638400 | tf_op jit(solution)/shard_map/all_gather | solution.py:137
  570.7 348.0 %reduce-scatter.23.cloned.1.call-start = ((), (), s32[]{:S(2)}) async-start(), calls=%async_computation.24 | async-start | bytes 3276800 | tf_op jit(solution)/shard_map/reduce_scatter | solution.py:141
  622.4 14.8 collective-permute-start.7
  623.0 34.5 %collective-permute-start.8 = (bf16[1,80,2048]{2,1,0:T(8,128)(2,1)S(1)}, bf16[1,80,2048]{2,1,0:T(8,128)(2,1)S(1)}, u32[]{:S(2)}, u32[]{:S(2)}) collective-permute-start(bf16[1,80,2048]{2,1,0:T(8,128)(2,1)S(1)} %get-tuple-element.85), channel_id=1, source_target_pairs={{0,3},{1,0},{2,1},{3,2},{4,7},{5,4},{6,5},{7,6},{8,11},{9,8},{10,9... | collective-permute-start | bytes 983048 | tf_op jit(solution)/shard_map/ppermute | solution.py:24
  628.4 207.7 %collective-permute-start.17 = (bf16[1,80,2048]{2,1,0:T(8,128)(2,1)}, bf16[1,80,2048]{2,1,0:T(8,128)(2,1)S(1)}, u32[]{:S(2)}, u32[]{:S(2)}) collective-permute-start(bf16[1,80,2048]{2,1,0:T(8,128)(2,1)} %get-tuple-element.93), channel_id=1, source_target_pairs={{0,1},{1,2},{2,3},{3,0},{4,5},{5,6},{6,7},{7,4},{8,9},{9,10},{10,1... | collective-permute-start | bytes 983048 | tf_op jit(solution)/shard_map/ppermute | solution.py:21
  637.2 38.5 %collective-permute-start.9 = (bf16[1,80,2048]{2,1,0:T(8,128)(2,1)S(1)}, bf16[1,80,2048]{2,1,0:T(8,128)(2,1)S(1)}, u32[]{:S(2)}, u32[]{:S(2)}) collective-permute-start(bf16[1,80,2048]{2,1,0:T(8,128)(2,1)S(1)} %collective-permute-done.7), channel_id=1, source_target_pairs={{0,1},{1,2},{2,3},{3,0},{4,5},{5,6},{6,7},{7,4},{8,9},{9,10},{10,1... | collective-permute-start | bytes 983048 | tf_op jit(solution)/shard_map/ppermute | solution.py:21
  832.6 140.0 %reduce-scatter.27.cloned.1.call-start = ((), (), s32[]{:S(2)}) async-start(), calls=%async_computation.27 | async-start | bytes 3276800 | tf_op jit(solution)/shard_map/reduce_scatter | solution.py:141
  832.6 28.7 %collective-permute-start.18 = (bf16[1,80,2048]{2,1,0:T(8,128)(2,1)}, bf16[1,80,2048]{2,1,0:T(8,128)(2,1)S(1)}, u32[]{:S(2)}, u32[]{:S(2)}) collective-permute-start(bf16[1,80,2048]{2,1,0:T(8,128)(2,1)} %get-tuple-element.93), channel_id=1, source_target_pairs={{0,3},{1,0},{2,1},{3,2},{4,7},{5,4},{6,5},{7,6},{8,11},{9,8},{10,9... | collective-permute-start | bytes 983048 | tf_op jit(solution)/shard_map/ppermute | solution.py:24
  836.1 29.6 %collective-permute-start.19 = (bf16[1,80,2048]{2,1,0:T(8,128)(2,1)S(1)}, bf16[1,80,2048]{2,1,0:T(8,128)(2,1)S(1)}, u32[]{:S(2)}, u32[]{:S(2)}) collective-permute-start(bf16[1,80,2048]{2,1,0:T(8,128)(2,1)S(1)} %collective-permute-done.17), channel_id=1, source_target_pairs={{0,1},{1,2},{2,3},{3,0},{4,5},{5,6},{6,7},{7,4},{8,9},{9,10},{10,1... | collective-permute-start | bytes 983048 | tf_op jit(solution)/shard_map/ppermute | solution.py:21
  889.8 136.9 %reduce-scatter.21.cloned.1.call-start = ((), (), s32[]{:S(2)}) async-start(), calls=%async_computation.23 | async-start | bytes 3276800 | tf_op jit(solution)/shard_map/reduce_scatter | solution.py:133
  896.8 177.3 %all-gather.25.cloned.1.call-start = ((), (), s32[]{:S(2)}) async-start(), calls=%async_computation.25 | async-start | bytes 1638400 | tf_op jit(solution)/shard_map/all_gather | solution.py:137
  1029.4 137.7 %all-gather.27.cloned.1.call-start = ((), (), s32[]{:S(2)}) async-start(), calls=%async_computation.28 | async-start | bytes 1638400 | tf_op jit(solution)/shard_map/all_gather | solution.py:137
  1074.0 492.4 %all-reduce.157.cloned.1.call-start = ((), (), s32[]{:S(2)}) async-start(), calls=%async_computation.38 | async-start | bytes 1310720 | tf_op jit(solution)/shard_map/psum | solution.py:328
  1305.7 46.3 %collective-permute-start.20 = (f32[1,640]{1,0:T(1,128)}, f32[1,640]{1,0:T(1,128)}, u32[]{:S(2)}, u32[]{:S(2)}) collective-permute-start(f32[1,640]{1,0:T(1,128)} %get-tuple-element.78), channel_id=1, source_target_pairs={{4,0},{8,4},{12,8},{5,1},{9,5},{13,9},{6,2},{10,6},{14,10},{7,3},{... | collective-permute-start | bytes 7688 | tf_op jit(solution)/shard_map/ppermute | solution.py:34
  1359.4 45.8 %collective-permute-start.22 = (f32[1,640]{1,0:T(1,128)S(1)}, f32[1,640]{1,0:T(1,128)S(1)}, u32[]{:S(2)}, u32[]{:S(2)}) collective-permute-start(f32[1,640]{1,0:T(1,128)S(1)} %multiply_add_fusion.39), channel_id=1, source_target_pairs={{4,0},{8,4},{12,8},{5,1},{9,5},{13,9},{6,2},{10,6},{14,10},{7,3},{... | collective-permute-start | bytes 7688 | tf_op jit(solution)/shard_map/ppermute | solution.py:34
  1363.2 42.1 %collective-permute-start.26 = (f32[1,640]{1,0:T(1,128)S(1)}, f32[1,640]{1,0:T(1,128)S(1)}, u32[]{:S(2)}, u32[]{:S(2)}) collective-permute-start(f32[1,640]{1,0:T(1,128)S(1)} %multiply_add_fusion.36), channel_id=1, source_target_pairs={{4,0},{8,4},{12,8},{5,1},{9,5},{13,9},{6,2},{10,6},{14,10},{7,3},{... | collective-permute-start | bytes 7688 | tf_op jit(solution)/shard_map/ppermute | solution.py:34
  1423.7 146.3 %reduce-scatter.37.cloned.1.call-start = ((), (), s32[]{:S(2)}) async-start(), calls=%async_computation.33 | async-start | bytes 7077888 | tf_op jit(solution)/shard_map/reduce_scatter | solution.py:312
  1435.4 175.9 %reduce-scatter.39.cloned.1.call-start = ((), (), s32[]{:S(2)}) async-start(), calls=%async_computation.34 | async-start | bytes 7077888 | tf_op jit(solution)/shard_map/reduce_scatter | solution.py:315
  1448.6 228.2 %reduce-scatter.41.cloned.1.call-start = ((), (), s32[]{:S(2)}) async-start(), calls=%async_computation.35 | async-start | bytes 7077888 | tf_op jit(solution)/shard_map/reduce_scatter | solution.py:321
  1460.4 263.4 %reduce-scatter.31.cloned.1.call-start = ((), (), s32[]{:S(2)}) async-start(), calls=%async_computation.30 | async-start | bytes 2949120 | tf_op jit(solution)/shard_map/reduce_scatter | solution.py:306
  1467.8 302.9 %reduce-scatter.35.cloned.1.call-start = ((), (), s32[]{:S(2)}) async-start(), calls=%async_computation.32 | async-start | bytes 2949120 | tf_op jit(solution)/shard_map/reduce_scatter | solution.py:318
  1474.3 343.4 %reduce-scatter.33.cloned.1.call-start = ((), (), s32[]{:S(2)}) async-start(), calls=%async_computation.31 | async-start | bytes 2949120 | tf_op jit(solution)/shard_map/reduce_scatter | solution.py:309
  1499.3 7.3 collective-permute-start.27
  1501.1 8.1 collective-permute-start.23
  1512.5 359.6 %reduce-scatter.25.cloned.1.call-start = ((), (), s32[]{:S(2)}) async-start(), calls=%async_computation.26 | async-start | bytes 3276800 | tf_op jit(solution)/shard_map/reduce_scatter | solution.py:141
  1519.5 406.6 %reduce-scatter.29.cloned.1.call-start = ((), (), s32[]{:S(2)}) async-start(), calls=%async_computation.29 | async-start | bytes 3276800 | tf_op jit(solution)/shard_map/reduce_scatter | solution.py:141
  1526.3 453.9 %reduce-scatter.17.cloned.1.call-start = ((), (), s32[]{:S(2)}) async-start(), calls=%async_computation.21 | async-start | bytes 3276800 | tf_op jit(solution)/shard_map/reduce_scatter | solution.py:133
  (203 other events, 5990.8 us)
Sparse Core Ops, SparseCore 0:
  9.9 32.8 all-gather.12
  44.7 30.1 all-gather.14
  76.8 30.5 all-gather.16
  432.7 51.2 reduce-scatter.14
  566.0 52.4 reduce-scatter.18
  620.5 54.2 all-gather.28
  676.6 44.8 all-gather.22
  723.4 45.5 all-gather.20
  770.9 45.5 all-gather.18
  818.4 45.2 all-gather.30
  866.0 52.5 reduce-scatter.22
  920.8 51.7 reduce-scatter.26
  974.9 51.7 reduce-scatter.20
  1029.5 32.3 all-gather.24
  1074.1 32.3 all-gather.26
  1423.9 57.4 all-reduce.156
  1485.0 61.1 reduce-scatter.36
  1549.5 61.8 reduce-scatter.38
  1615.1 61.7 reduce-scatter.40
  1680.0 43.6 reduce-scatter.30
  1727.1 43.6 reduce-scatter.34
  1774.0 43.6 reduce-scatter.32
  1820.0 52.0 reduce-scatter.24
  1874.3 51.7 reduce-scatter.28
  1928.4 51.7 reduce-scatter.16
